TPU v7x, 32 devices: a whole 2x2x4 slice. The times are simulated.
32 devices in a mesh: shard: 4 (over z), ctx: 4 (over x, core), tp: 2 (over y).
Axes of the slice: x: 2, y: 2, z: 4, core: 2. Of those that a mesh axis runs over, the one named last changes fastest.
Arguments:
- hidden_in: bfloat16 [4, 1024, 1024], P('shard', 'ctx'), may hold values from -6 to 6
- out_grad: bfloat16 [4, 1024, 1024], P('shard', 'ctx'), may hold values from -6 to 6
- segment_ids: int32 [4, 1024], P('shard'), may hold values from 0 to 3, never falling along the last dimension, each value on 1 to 512 neighbouring positions
- w_qkv: bfloat16 [3, 1024, 1024], P(None, 'shard', 'tp'), may hold values from -0.1875 to 0.1875
- bias_qv: float32 [2, 1024], P(None, 'tp'), may hold values from -3 to 3
- w_out: bfloat16 [1024, 1024], P('tp', 'shard'), may hold values from -0.75 to 0.75
- bias_out: float32 [1024], replicated, may hold values from -3 to 3
- norm1_gain: float32 [1024], replicated, may hold values from 0.5 to 1.5
- norm1_shift: float32 [1024], replicated, may hold values from -3 to 3
- w_up: bfloat16 [1024, 4096], P('shard', 'tp'), may hold values from -0.1875 to 0.1875
- bias_up: float32 [4096], P('tp'), may hold values from -3 to 3
- w_down: bfloat16 [4096, 1024], P('tp', 'shard'), may hold values from -0.09375 to 0.09375
- bias_down: float32 [1024], replicated, may hold values from -3 to 3
- norm2_gain: float32 [1024], replicated, may hold values from 0.5 to 1.5
- norm2_shift: float32 [1024], replicated, may hold values from -3 to 3
Outputs:
- output: bfloat16 [4, 1024, 1024], P('shard', 'ctx')
- input_grad: bfloat16 [4, 1024, 1024], P('shard', 'ctx')
- w_qkv_grad: float32 [3, 1024, 1024], P(None, 'shard', 'tp')
- bias_qv_grad: float32 [2, 1024], P(None, 'tp')
- w_out_grad: float32 [1024, 1024], P('tp', 'shard')
- bias_out_grad: float32 [1024], replicated
- norm1_gain_grad: float32 [1024], replicated
- norm1_shift_grad: float32 [1024], replicated
- w_up_grad: float32 [1024, 4096], P('shard', 'tp')
- bias_up_grad: float32 [4096], P('tp')
- w_down_grad: float32 [4096, 1024], P('tp', 'shard')
- bias_down_grad: float32 [1024], replicated
- norm2_gain_grad: float32 [1024], replicated
- norm2_shift_grad: float32 [1024], replicated
Inputs may be any that keep to these rules, and one draw needn't show every extreme that they name: `segment_ids`: within each sequence the ids never fall and start at 0; each document has at most 512 tokens, and some document has exactly that many.
All inputs are finite; a program needn't handle non-finite values.
Results may differ from a plain program's by a relative error of at most 0.022.
The roundings to bfloat16 on the way count: a program that leaves them out, or rounds other values in their place, can miss the bound.
Values may be sent and summed in bfloat16 or wider, within the bound.
A program may use at most 128 MiB of HBM per device.

v0:
```python
import math
import jax
import jax.numpy as jnp
from jax import lax
from jax.sharding import PartitionSpec as P

HEADS = 16
EPSILON = 1e-05


def normalize(resid, gain, shift):
    average = jnp.mean(resid, axis=-1, keepdims=True)
    centred = resid - average
    variance = jnp.mean(centred * centred, axis=-1, keepdims=True)
    inv_std = lax.rsqrt(variance + EPSILON)
    normed = centred * inv_std
    return (normed * gain + shift, normed, inv_std)


def normalize_back(cotan, normed, inv_std, gain):
    scaled = cotan * gain
    return inv_std * (
        scaled
        - jnp.mean(scaled, axis=-1, keepdims=True)
        - normed * jnp.mean(scaled * normed, axis=-1, keepdims=True)
    )


def gelu_value(pre_act):
    return 0.5 * pre_act * (1.0 + jax.scipy.special.erf(pre_act * 0.7071067811865476))


def gelu_slope(pre_act):
    return (
        0.5 * (1.0 + jax.scipy.special.erf(pre_act * 0.7071067811865476))
        + pre_act * jnp.exp(-0.5 * pre_act * pre_act) * 0.3989422804014327
    )


def block_scores(query_block, keys, ids_block, ids_whole, scale):
    scores = (
        jnp.einsum("qhe,khe->hqk", query_block, keys, preferred_element_type=jnp.float32) * scale
    )
    return jnp.where((ids_block[:, None] == ids_whole[None, :])[None], scores, -jnp.inf)


GROUP = ("ctx", "tp")


def dot_t(left, right):
    return lax.dot_general(
        left, right, (((1,), (1,)), ((), ())), preferred_element_type=jnp.float32
    )


def dot_rows(left, right):
    return lax.dot_general(
        left, right, (((0,), (0,)), ((), ())), preferred_element_type=jnp.float32
    )


def dot(left, right):
    return jnp.dot(left, right, preferred_element_type=jnp.float32)


def spread(part):
    return lax.all_gather(part, GROUP, axis=1, tiled=True)


def collect(whole):
    return lax.psum_scatter(whole, GROUP, scatter_dimension=1, tiled=True).astype(jnp.float32)


def shards(
    hidden_in,
    out_grad,
    segment_ids,
    w_qkv,
    bias_qv,
    w_out,
    bias_out,
    norm1_gain,
    norm1_shift,
    w_up,
    bias_up,
    w_down,
    bias_down,
    norm2_gain,
    norm2_shift,
):
    seq_count, local_len, width = hidden_in.shape
    ctx_count = lax.axis_size("ctx")
    tp_count = lax.axis_size("tp")
    ctx_at = lax.axis_index("ctx")
    tp_at = lax.axis_index("tp")
    full_len = local_len * ctx_count
    part_len = local_len // tp_count
    row_count = seq_count * full_len
    head_dim = width // HEADS
    scale = 1.0 / math.sqrt(head_dim)
    owned_rows = w_up.shape[0]
    cols = w_qkv.shape[2] // ctx_count
    units = w_up.shape[1] // ctx_count
    local_heads = cols // head_dim
    block_rows = min(512, full_len)
    block_count = full_len // block_rows

    def mine(array, size, axis):
        return lax.dynamic_slice_in_dim(array, ctx_at * size, size, axis)

    qkv_own = mine(w_qkv, cols, 2).transpose(1, 0, 2).reshape(owned_rows, 3 * cols)
    qkv_full = lax.all_gather(qkv_own, "shard", axis=0, tiled=True)
    tokens_all = lax.all_gather(hidden_in, "ctx", axis=1, tiled=True).reshape(row_count, width)
    rest_own = jnp.concatenate(
        [mine(w_out, cols, 0).T, mine(w_up, units, 1), mine(w_down, units, 0).T], axis=1
    )
    rest_full = lax.all_gather(rest_own, "shard", axis=0, tiled=True)
    out_full = rest_full[:, :cols]
    up_full = rest_full[:, cols : cols + units]
    down_full = rest_full[:, cols + units :]
    bias_own = mine(bias_qv, cols, 1)
    bias_three = jnp.concatenate([bias_own[0], jnp.zeros_like(bias_own[0]), bias_own[1]])
    project = (dot(tokens_all, qkv_full) + bias_three).astype(jnp.bfloat16)
    heads = project.reshape(seq_count, full_len, 3, local_heads, head_dim)

    def attend_sequence(packed):
        seq_heads, seq_ids = packed
        keys = seq_heads[:, 1]
        values = seq_heads[:, 2]
        queries = seq_heads[:, 0].reshape(block_count, block_rows, local_heads, head_dim)
        id_blocks = seq_ids.reshape(block_count, block_rows)

        def attend_block(piece):
            query_block, ids_block = piece
            scores = block_scores(query_block, keys, ids_block, seq_ids, scale)
            log_total = jax.nn.logsumexp(scores, axis=-1)
            probs_low = jnp.exp(scores - log_total[..., None]).astype(jnp.bfloat16)
            attended = jnp.einsum(
                "hqk,khe->qhe", probs_low, values, preferred_element_type=jnp.float32
            ).astype(jnp.bfloat16)
            return (attended, log_total)

        attended, log_total = lax.map(attend_block, (queries, id_blocks))
        return (attended.reshape(full_len, local_heads, head_dim), log_total)

    attended_heads, log_totals = lax.map(attend_sequence, (heads, segment_ids))
    attended = attended_heads.reshape(row_count, cols)

    def whole(part):
        return part.astype(jnp.bfloat16).reshape(seq_count, full_len, width)

    def part_of(array):
        return lax.dynamic_slice_in_dim(array, tp_at * part_len, part_len, 1)

    resid_one = (
        collect(whole(dot_t(attended, out_full)))
        + bias_out
        + part_of(hidden_in).astype(jnp.float32)
    )
    first, normed_one, inv_one = normalize(resid_one, norm1_gain, norm1_shift)
    first_all = spread(first.astype(jnp.bfloat16)).reshape(row_count, width)
    pre_act = dot(first_all, up_full) + mine(bias_up, units, 0)
    activated = gelu_value(pre_act).astype(jnp.bfloat16)
    resid_two = collect(whole(dot_t(activated, down_full))) + bias_down + first
    result, normed_two, inv_two = normalize(resid_two, norm2_gain, norm2_shift)
    grad_float = part_of(out_grad).astype(jnp.float32)

    def total(array):
        return jnp.sum(array, axis=(0, 1))

    gain_two_grad = total(grad_float * normed_two)
    shift_two_grad = total(grad_float)
    resid_two_grad = normalize_back(grad_float, normed_two, inv_two, norm2_gain)
    two_all = spread(resid_two_grad.astype(jnp.bfloat16)).reshape(row_count, width)
    output = lax.all_gather(result.astype(jnp.bfloat16), "tp", axis=1, tiled=True)
    bias_down_grad = total(resid_two_grad)
    pre_grad = dot(two_all, down_full) * gelu_slope(pre_act)
    pre_low = pre_grad.astype(jnp.bfloat16)
    bias_up_grad = jnp.sum(pre_grad, axis=0)
    first_grad = resid_two_grad + collect(whole(dot_t(pre_low, up_full)))
    part_ffn = jnp.concatenate(
        [dot_rows(first_all, pre_low), dot_rows(two_all, activated)], axis=1
    ).astype(jnp.bfloat16)
    gain_one_grad = total(first_grad * normed_one)
    shift_one_grad = total(first_grad)
    resid_one_grad = normalize_back(first_grad, normed_one, inv_one, norm1_gain)
    bias_out_grad = total(resid_one_grad)
    one_all = spread(resid_one_grad.astype(jnp.bfloat16)).reshape(row_count, width)
    attended_grad = dot(one_all, out_full).astype(jnp.bfloat16)
    grad_heads = attended_grad.reshape(seq_count, full_len, local_heads, head_dim)

    def back_sequence(packed):
        seq_heads, seq_ids, seq_attended, seq_grad, seq_log = packed
        keys = seq_heads[:, 1]
        values = seq_heads[:, 2]
        queries = seq_heads[:, 0].reshape(block_count, block_rows, local_heads, head_dim)
        id_blocks = seq_ids.reshape(block_count, block_rows)
        att_blocks = seq_attended.reshape(block_count, block_rows, local_heads, head_dim)
        grad_blocks = seq_grad.reshape(block_count, block_rows, local_heads, head_dim)

        def back_block(carry, piece):
            key_total, value_total = carry
            query_block, ids_block, att_block, grad_block, log_block = piece
            scores = block_scores(query_block, keys, ids_block, seq_ids, scale)
            probs = jnp.exp(scores - log_block[..., None])
            probs_low = probs.astype(jnp.bfloat16)
            prob_grad = jnp.einsum(
                "qhe,khe->hqk", grad_block, values, preferred_element_type=jnp.float32
            )
            offset = jnp.sum(
                grad_block.astype(jnp.float32) * att_block.astype(jnp.float32), axis=-1
            ).T
            score_grad = (probs * (prob_grad - offset[..., None]) * scale).astype(jnp.bfloat16)
            query_grad = jnp.einsum(
                "hqk,khe->qhe", score_grad, keys, preferred_element_type=jnp.float32
            ).astype(jnp.bfloat16)
            key_total = key_total + jnp.einsum(
                "hqk,qhe->khe", score_grad, query_block, preferred_element_type=jnp.float32
            )
            value_total = value_total + jnp.einsum(
                "hqk,qhe->khe", probs_low, grad_block, preferred_element_type=jnp.float32
            )
            return ((key_total, value_total), query_grad)

        empty = jnp.zeros((full_len, local_heads, head_dim), jnp.float32)
        (key_total, value_total), query_grads = lax.scan(
            back_block, (empty, empty), (queries, id_blocks, att_blocks, grad_blocks, seq_log)
        )
        return jnp.stack(
            [
                query_grads.reshape(full_len, local_heads, head_dim),
                key_total.astype(jnp.bfloat16),
                value_total.astype(jnp.bfloat16),
            ],
            axis=1,
        )

    head_grads = lax.map(
        back_sequence, (heads, segment_ids, attended_heads, grad_heads, log_totals)
    )
    proj_grad = head_grads.reshape(row_count, 3 * cols)
    proj_sum = jnp.sum(proj_grad.astype(jnp.float32), axis=0)
    bias_qv_grad = jnp.concatenate([proj_sum[:cols], proj_sum[2 * cols :]])
    input_part = resid_one_grad + collect(whole(dot_t(proj_grad, qkv_full)))
    input_grad = lax.all_gather(input_part.astype(jnp.bfloat16), "tp", axis=1, tiled=True)
    part_attn = jnp.concatenate(
        [dot_rows(tokens_all, proj_grad), dot_rows(one_all, attended)], axis=1
    ).astype(jnp.bfloat16)

    def owned(part):
        mean = lax.psum_scatter(part, "shard", scatter_dimension=0, tiled=True)
        return lax.all_gather(mean, "ctx", axis=0).astype(jnp.float32)

    own_ffn = owned(part_ffn)
    own_attn = owned(part_attn)
    up_grad = own_ffn[:, :, :units].transpose(1, 0, 2).reshape(w_up.shape)
    down_grad = own_ffn[:, :, units:].transpose(0, 2, 1).reshape(w_down.shape)
    qkv_grad = (
        own_attn[:, :, : 3 * cols]
        .reshape(ctx_count, owned_rows, 3, cols)
        .transpose(2, 1, 0, 3)
        .reshape(w_qkv.shape)
    )
    out_weight_grad = own_attn[:, :, 3 * cols :].transpose(0, 2, 1).reshape(w_out.shape)
    sliced = jnp.concatenate([bias_qv_grad, bias_up_grad])
    slots = jnp.zeros((tp_count, ctx_count, sliced.shape[0]), jnp.float32)
    slots = lax.dynamic_update_slice(slots, sliced[None, None], (tp_at, ctx_at, 0))
    small = lax.psum(
        jnp.concatenate(
            [
                bias_out_grad,
                gain_one_grad,
                shift_one_grad,
                bias_down_grad,
                gain_two_grad,
                shift_two_grad,
                slots.reshape(-1),
            ]
        ),
        ("shard", "ctx", "tp"),
    )
    sums = small[: 6 * width].reshape(6, width)
    slots = small[6 * width :].reshape(tp_count, ctx_count, -1)
    slots = lax.dynamic_index_in_dim(slots, tp_at, 0, keepdims=False)
    bias_qv_total = (
        slots[:, : 2 * cols].reshape(ctx_count, 2, cols).transpose(1, 0, 2).reshape(bias_qv.shape)
    )
    return (
        output,
        input_grad,
        qkv_grad,
        bias_qv_total,
        out_weight_grad,
        sums[0],
        sums[1],
        sums[2],
        up_grad,
        slots[:, 2 * cols :].reshape(bias_up.shape),
        down_grad,
        sums[3],
        sums[4],
        sums[5],
    )


def solution(mesh):
    return jax.shard_map(
        shards,
        mesh=mesh,
        in_specs=(
            P("shard", "ctx", None),
            P("shard", "ctx", None),
            P("shard", None),
            P(None, "shard", "tp"),
            P(None, "tp"),
            P("tp", "shard"),
            P(),
            P(),
            P(),
            P("shard", "tp"),
            P("tp"),
            P("tp", "shard"),
            P(),
            P(),
            P(),
        ),
        out_specs=(
            P("shard", "ctx", None),
            P("shard", "ctx", None),
            P(None, "shard", "tp"),
            P(None, "tp"),
            P("tp", "shard"),
            P(),
            P(),
            P(),
            P("shard", "tp"),
            P("tp"),
            P("tp", "shard"),
            P(),
            P(),
            P(),
        ),
        check_vma=False,
    )
```

profile of v0, /device:TPU:0, one launch (start us, length us, event | category | flops | bytes accessed | tf_op | source)
XLA Modules:
  0.0 506.4 jit_solution(6332370861797403989)
XLA Ops:
  14.3 21.3 %all_gather.36 = bf16[1024,384]{0,1:T(8,128)(2,1)S(1)} all-gather(bf16[256,384]{0,1:T(8,128)(2,1)S(1)} %bitcast.238), channel_id=1, replica_groups=mesh['shard'=4,'ctx'=4,'tp'=2] {'shard'}, dimensions={0}, use_global_device_ids=true | all-gather | bytes 983040 | tf_op jit(solution)/shard_map/all_gather | solution.py:112
  35.7 2.6 add_convert_fusion
  38.6 7.9 %while.45 = (s32[]{:T(128)}, bf16[2,512,2,64]{1,3,2,0:T(8,128)(2,1)S(1)}, f32[2,2,512]{2,1,0:T(2,128)S(1)}, s32[2,512]{1,0:T(2,128)S(1)}, s32[1024]{0:T(1024)S(1...) while((s32[]{:T(128)}, ...), condition=%wide.region_3.4_spmd, body=%wide.region_0.3_spmd.sunk | while | flops 280567808 | bytes 15526005 | solution.py:143
  46.8 40.8 %all-gather.12.cloned.1.call-done = bf16[1024,1152]{0,1:T(8,128)(2,1)} async-done(((bf16[256,1152]{0,1:T(8,128)(2,1)}), bf16[1024,1152]{0,1:T(8,128)(2,1)}) %all-gather.12.cloned.1.call-update) | async-done | bytes 2359312 | tf_op jit(solution)/shard_map/all_gather | solution.py:117
  87.6 3.1 convert_bitcast_fusion.3
  90.8 40.0 %reduce-scatter.7.cloned.1.call-done = bf16[1,128,1024]{2,1,0:T(8,128)(2,1)} async-done(((bf16[1,1024,1024]{2,1,0:T(8,128)(2,1)}), bf16[1,128,1024]{2,1,0:T(8,128)(2,1)}) %reduce-scatter.7.cloned.1.call-update) | async-done | bytes 262160 | tf_op jit(solution)/shard_map/reduce_scatter | solution.py:71
  135.8 27.1 %all-gather.14.cloned.1.call-done = bf16[1,1024,1024]{2,1,0:T(8,128)(2,1)} async-done(((bf16[1,128,1024]{2,1,0:T(8,128)(2,1)}), bf16[1,1024,1024]{2,1,0:T(8,128)(2,1)}) %all-gather.14.cloned.1.call-update) | async-done | bytes 2097168 | tf_op jit(solution)/shard_map/all_gather | solution.py:67
  162.9 4.6 multiply_convert_fusion.1
  168.4 3.8 convert_bitcast_fusion.2
  172.3 41.2 %reduce-scatter.9.cloned.1.call-done = bf16[1,128,1024]{2,1,0:T(8,128)(2,1)} async-done(((bf16[1,1024,1024]{2,1,0:T(8,128)(2,1)}), bf16[1,128,1024]{2,1,0:T(8,128)(2,1)}) %reduce-scatter.9.cloned.1.call-update) | async-done | bytes 262160 | tf_op jit(solution)/shard_map/reduce_scatter | solution.py:71
  216.6 27.7 %all-gather.16.cloned.1.call-done = bf16[1,1024,1024]{2,1,0:T(8,128)(2,1)} async-done(((bf16[1,128,1024]{2,1,0:T(8,128)(2,1)}), bf16[1,1024,1024]{2,1,0:T(8,128)(2,1)}) %all-gather.16.cloned.1.call-update) | async-done | bytes 2097168 | tf_op jit(solution)/shard_map/all_gather | solution.py:67
  244.3 4.5 fusion.111
  249.8 3.8 convert_bitcast_fusion.1
  253.7 41.2 %reduce-scatter.11.cloned.1.call-done = bf16[1,128,1024]{2,1,0:T(8,128)(2,1)} async-done(((bf16[1,1024,1024]{2,1,0:T(8,128)(2,1)}), bf16[1,128,1024]{2,1,0:T(8,128)(2,1)}) %reduce-scatter.11.cloned.1.call-update) | async-done | bytes 262160 | tf_op jit(solution)/shard_map/reduce_scatter | solution.py:71
  299.1 3.3 fusion.72
  305.5 21.4 %all-gather.18.cloned.1.call-done = bf16[1,1024,1024]{2,1,0:T(8,128)(2,1)} async-done(((bf16[1,128,1024]{2,1,0:T(8,128)(2,1)}), bf16[1,1024,1024]{2,1,0:T(8,128)(2,1)}) %all-gather.18.cloned.1.call-update) | async-done | bytes 2097168 | tf_op jit(solution)/shard_map/all_gather | solution.py:67
  326.9 2.3 fusion.81
  329.9 12.5 %while.46 = (s32[]{:T(128)}, f32[1024,2,64]{0,2,1:T(8,128)S(1)}, f32[1024,2,64]{0,2,1:T(8,128)}, bf16[2,512,2,64]{1,3,2,0:T(8,128)(2,1)S(1)}, bf16[2,512,2,64]{1...) while((s32[]{:T(128)}, f32[1024,2,64]{0,2,1:T(8,128)S(1)}, ...), condition=%wide.region_17.18_spmd.clone, body=%wide.region_15.17_spmd.clone.sunk | while | flops 683998208 | bytes 29526284 | solution.py:226
  344.2 2.2 fusion.84
  348.4 25.0 %reduce-scatter.17.cloned.1.call-done = bf16[256,1024]{0,1:T(8,128)(2,1)} async-done(((bf16[1024,1024]{0,1:T(8,128)(2,1)}), bf16[256,1024]{0,1:T(8,128)(2,1)}) %reduce-scatter.17.cloned.1.call-update) | async-done | bytes 524304 | tf_op jit(solution)/shard_map/reduce_scatter | solution.py:251
  373.5 2.6 convert_bitcast_fusion
  376.2 8.4 %all_gather.40 = bf16[1,256,1024]{2,1,0:T(8,128)(2,1)} all-gather(bf16[1,128,1024]{2,1,0:T(8,128)(2,1)S(1)} %get-tuple-element.297), channel_id=1, replica_groups=mesh['shard'=4,'ctx'=4,'tp'=2] {'tp'}, dimensions={1}, use_global_device_ids=true | all-gather | bytes 786432 | tf_op jit(solution)/shard_map/all_gather | solution.py:175
  385.0 17.8 %reduce-scatter.15.cloned.1.call-done = bf16[256,512]{0,1:T(8,128)(2,1)} async-done(((bf16[1024,512]{0,1:T(8,128)(2,1)}), bf16[256,512]{0,1:T(8,128)(2,1)}) %reduce-scatter.15.cloned.1.call-update) | async-done | bytes 262160 | tf_op jit(solution)/shard_map/reduce_scatter | solution.py:251
  402.8 39.6 %psum.7 = f32[12288]{0:T(1024)S(1)} all-reduce(f32[12288]{0:T(1024)S(1)} %constant_dynamic-update-slice_fusion), channel_id=1, replica_groups=mesh['shard'=4,'ctx'=4,'tp'=2] {'shard','ctx','tp'}, use_global_device_ids=true, to_apply=%region_28.29 | all-reduce | flops 12288 | bytes 98304 | tf_op jit(solution)/shard_map/psum | solution.py:268
  444.3 5.0 reshape.372
  449.3 4.5 slice_bitcast_fusion
  455.5 2.9 copy.45
  458.4 2.2 copy.53
  460.6 9.5 %reduce-scatter.13.cloned.1.call-done = bf16[1,128,1024]{2,1,0:T(8,128)(2,1)} async-done(((bf16[1,1024,1024]{2,1,0:T(8,128)(2,1)}), bf16[1,128,1024]{2,1,0:T(8,128)(2,1)}) %reduce-scatter.13.cloned.1.call-update) | async-done | bytes 262160 | tf_op jit(solution)/shard_map/reduce_scatter | solution.py:71
  471.1 8.6 %all_gather.43 = bf16[1,256,1024]{2,1,0:T(8,128)(2,1)} all-gather(bf16[1,128,1024]{2,1,0:T(8,128)(2,1)S(1)} %add_convert_fusion.1), channel_id=1, replica_groups=mesh['shard'=4,'ctx'=4,'tp'=2] {'tp'}, dimensions={1}, use_global_device_ids=true | all-gather | bytes 786432 | tf_op jit(solution)/shard_map/all_gather | solution.py:245
  479.7 8.7 %all-gather.20.cloned.1.call-done = bf16[1024,512]{0,1:T(8,128)(2,1)} async-done(((bf16[256,512]{0,1:T(8,128)(2,1)}), bf16[1024,512]{0,1:T(8,128)(2,1)}) %all-gather.20.cloned.1.call-update) | async-done | bytes 1048592 | tf_op jit(solution)/shard_map/all_gather | solution.py:252
  496.3 2.0 copy.44
  (205 shorter events, 63.9 us)
Async XLA Ops:
  7.2 5.3 %copy-start.12 = (s32[1,1024]{1,0:T(1,128)S(1)}, s32[1,1024]{1,0:T(1,128)}, u32[]{:S(2)}) copy-start(s32[1,1024]{1,0:T(1,128)} %param.21) | copy-start | bytes 12292
  7.2 28.5 %all-gather.10.cloned.1.call-start = ((), (), s32[]{:S(2)}) async-start(), calls=%async_computation.6 | async-start | bytes 2621440 | tf_op jit(solution)/shard_map/all_gather | solution.py:113
  7.9 79.7 %all-gather.12.cloned.1.call-start = ((), (), s32[]{:S(2)}) async-start(), calls=%async_computation.7 | async-start | bytes 2949120 | tf_op jit(solution)/shard_map/all_gather | solution.py:117
  11.3 119.5 %reduce-scatter.7.cloned.1.call-start = ((), (), s32[]{:S(2)}) async-start(), calls=%async_computation.8 | async-start | bytes 2359296 | tf_op jit(solution)/shard_map/reduce_scatter | solution.py:71
  46.5 44.2 %copy-start.13 = (bf16[1024,2,64]{0,2,1:T(8,128)(2,1)}, bf16[1024,2,64]{0,2,1:T(8,128)(2,1)S(1)}, u32[]{:S(2)}) copy-start(bf16[1024,2,64]{0,2,1:T(8,128)(2,1)S(1)} %get-tuple-element.588) | copy-start | bytes 786436
  87.6 43.2 %copy-start.3 = (bf16[1,256,1024]{2,1,0:T(8,128)(2,1)S(1)}, bf16[1,256,1024]{2,1,0:T(8,128)(2,1)}, u32[]{:S(2)}) copy-start(bf16[1,256,1024]{2,1,0:T(8,128)(2,1)} %param.19) | copy-start | bytes 1572868
  87.6 43.2 %copy-start.15 = (f32[1024]{0:T(1024)S(1)}, f32[1024]{0:T(1024)}, u32[]{:S(2)}) copy-start(f32[1024]{0:T(1024)} %param.25) | copy-start | bytes 12292
  90.7 42.4 %copy-start.16 = (f32[1024]{0:T(1024)S(1)}, f32[1024]{0:T(1024)}, u32[]{:S(2)}) copy-start(f32[1024]{0:T(1024)} %param.26) | copy-start | bytes 12292
  90.7 42.4 %copy-start.17 = (f32[1024]{0:T(1024)S(1)}, f32[1024]{0:T(1024)}, u32[]{:S(2)}) copy-start(f32[1024]{0:T(1024)} %param.27) | copy-start | bytes 12292
  90.7 72.2 %all-gather.14.cloned.1.call-start = ((), (), s32[]{:S(2)}) async-start(), calls=%async_computation.9 | async-start | bytes 2359296 | tf_op jit(solution)/shard_map/all_gather | solution.py:67
  134.9 78.6 %reduce-scatter.9.cloned.1.call-start = ((), (), s32[]{:S(2)}) async-start(), calls=%async_computation.10 | async-start | bytes 2359296 | tf_op jit(solution)/shard_map/reduce_scatter | solution.py:71
  172.2 41.3 %copy-start.2 = (bf16[1,128,1024]{2,1,0:T(8,128)(2,1)S(1)}, bf16[1,128,1024]{2,1,0:T(8,128)(2,1)}, u32[]{:S(2)}) copy-start(bf16[1,128,1024]{2,1,0:T(8,128)(2,1)} %reduce-scatter.7.cloned.1.call-done) | copy-start | bytes 786436
  172.2 41.3 %copy-start.19 = (f32[1024]{0:T(1024)S(1)}, f32[1024]{0:T(1024)}, u32[]{:S(2)}) copy-start(f32[1024]{0:T(1024)} %param.31) | copy-start | bytes 12292
  172.2 42.8 %copy-start.10 = (bf16[1,256,1024]{2,1,0:T(8,128)(2,1)S(1)}, bf16[1,256,1024]{2,1,0:T(8,128)(2,1)}, u32[]{:S(2)}) copy-start(bf16[1,256,1024]{2,1,0:T(8,128)(2,1)} %param.20) | copy-start | bytes 1572868
  172.2 42.8 %copy-start.18 = (f32[1024]{0:T(1024)S(1)}, f32[1024]{0:T(1024)}, u32[]{:S(2)}) copy-start(f32[1024]{0:T(1024)} %param.32) | copy-start | bytes 12292
  172.2 43.1 %copy-start.20 = (f32[1024]{0:T(1024)S(1)}, f32[1024]{0:T(1024)}, u32[]{:S(2)}) copy-start(f32[1024]{0:T(1024)} %param.33) | copy-start | bytes 12292
  172.3 72.0 %all-gather.16.cloned.1.call-start = ((), (), s32[]{:S(2)}) async-start(), calls=%async_computation.11 | async-start | bytes 2359296 | tf_op jit(solution)/shard_map/all_gather | solution.py:67
  216.4 78.5 %reduce-scatter.11.cloned.1.call-start = ((), (), s32[]{:S(2)}) async-start(), calls=%async_computation.12 | async-start | bytes 2359296 | tf_op jit(solution)/shard_map/reduce_scatter | solution.py:71
  253.6 73.3 %all-gather.18.cloned.1.call-start = ((), (), s32[]{:S(2)}) async-start(), calls=%async_computation.13 | async-start | bytes 2359296 | tf_op jit(solution)/shard_map/all_gather | solution.py:67
  299.0 74.5 %reduce-scatter.17.cloned.1.call-start = ((), (), s32[]{:S(2)}) async-start(), calls=%async_computation.16 | async-start | bytes 2621440 | tf_op jit(solution)/shard_map/reduce_scatter | solution.py:251
  299.1 3.3 copy-start.22
  299.1 3.3 copy-start.25
  305.3 97.5 %reduce-scatter.15.cloned.1.call-start = ((), (), s32[]{:S(2)}) async-start(), calls=%async_computation.15 | async-start | bytes 1310720 | tf_op jit(solution)/shard_map/reduce_scatter | solution.py:251
  332.8 2.0 copy-start.9
  344.0 2.4 copy-start.21
  348.4 95.9 %all-gather.22.cloned.1.call-start = ((), (), s32[]{:S(2)}) async-start(), calls=%async_computation.18 | async-start | bytes 2621440 | tf_op jit(solution)/shard_map/all_gather | solution.py:252
  373.5 96.6 %reduce-scatter.13.cloned.1.call-start = ((), (), s32[]{:S(2)}) async-start(), calls=%async_computation.14 | async-start | bytes 2359296 | tf_op jit(solution)/shard_map/reduce_scatter | solution.py:71
  376.2 112.3 %all-gather.20.cloned.1.call-start = ((), (), s32[]{:S(2)}) async-start(), calls=%async_computation.17 | async-start | bytes 1310720 | tf_op jit(solution)/shard_map/all_gather | solution.py:252
  458.4 11.7 %copy-start.5 = (f32[1,128,1024]{2,1,0:T(8,128)S(1)}, f32[1,128,1024]{2,1,0:T(8,128)}, u32[]{:S(2)}) copy-start(f32[1,128,1024]{2,1,0:T(8,128)} %copy-done.4) | copy-start | bytes 1572868
  494.5 3.8 copy-start.6
  494.5 5.4 %copy-start.1 = (bf16[256,2048]{1,0:T(8,128)(2,1)S(1)}, bf16[256,2048]{1,0:T(8,128)(2,1)}, u32[]{:S(2)}) copy-start(bf16[256,2048]{1,0:T(8,128)(2,1)} %param.28) | copy-start | bytes 3145732
  496.3 2.8 copy-start.7
  (10 other events, 12.7 us)
Sparse Core Ops, SparseCore 0:
  9.6 25.2 all-gather.9
  37.0 50.5 all-gather.11
  91.5 39.2 reduce-scatter.6
  135.1 27.7 all-gather.13
  172.4 41.0 reduce-scatter.8
  216.5 27.7 all-gather.15
  253.7 41.0 reduce-scatter.10
  299.1 27.7 all-gather.17
  329.8 43.6 reduce-scatter.16
  376.2 26.4 reduce-scatter.14
  404.3 21.4 all-gather.21
  428.9 41.1 reduce-scatter.12
  471.6 16.7 all-gather.19
where the time goes:
time: 507 us; the launch traced here: 506 us
  waiting for transfers between devices  301 us (59%)
  blocking collectives  78 us (15%)
  matrix products  50.5 us (10%)
  local copies, waits for them, and re-layouts  40.4 us (8%)
  other arithmetic  20.5 us (4%)
  between operations  14.5 us (3%)
    reduce_scatter x4, waiting for transfers between devices, collect(): lax.psum_scatter(whole, GROUP, scatter_dimension=1, tiled=True)  132 us
    all_gather x3, waiting for transfers between devices, spread(): return lax.all_gather(part, GROUP, axis=1, tiled=True)  76.2 us
    reduce_scatter x2, waiting for transfers between devices, owned(): mean = lax.psum_scatter(part, 'shard', scatter_dimension=0, tiled=True)  42.8 us
    all_gather x1, waiting for transfers between devices, shards(): rest_full = lax.all_gather(rest_own, 'shard', axis=0, tiled=True)  40.8 us
    psum x1, blocking collectives, shards(): lax.psum(jnp.concatenate([bias_out_grad, gain_one_grad, shift_one_grad, b...  39.6 us
    all_gather x1, blocking collectives, shards(): qkv_full = lax.all_gather(qkv_own, 'shard', axis=0, tiled=True)  21.3 us
    dot_general x4, matrix products, dot(): return jnp.dot(left, right, preferred_element_type=jnp.float32)  14 us
    dot_general x4, matrix products, dot_t(): lax.dot_general(left, right, (((1,), (1,)), ((), ())), preferred_element_...  13.3 us
  transfers between devices with their start and end apart: 13, of which 11 were waited for; matrix products, arithmetic and copies ran while one was open for 13% of the time, Pallas kernels for 0%

commit v1 on v0

--- a/solution.py
+++ b/solution.py
@@ -6,6 +6,26 @@
 
 HEADS = 16
 EPSILON = 1e-05
+
+
+def lay_the_sources_all(inp, dim_at):
+    inp = jnp.moveaxis(inp, 0, dim_at)
+    heard = inp.shape
+    return inp.reshape(*heard[:dim_at], heard[dim_at] * heard[dim_at + 1], *heard[dim_at + 2 :])
+
+
+def settle_sizes_by_axis(m, axis_key):
+    count_all = lax.axis_size(axis_key)
+    s_next = m[None]
+    for nth in range(count_all.bit_length() - 1):
+        r1 = 1 << nth
+        mixed_arr = lax.ppermute(
+            s_next, axis_name=axis_key, perm=[(p, p ^ r1) for p in range(count_all)]
+        )
+        extra = jnp.stack([s_next, mixed_arr], axis=0)
+        block_now = lax.axis_index(axis_key) >> nth & 1
+        s_next = jnp.where(block_now == 0, extra, extra[::-1]).reshape(-1, *m.shape)
+    return s_next
 
 
 def normalize(resid, gain, shift):
@@ -88,6 +108,10 @@
     norm2_gain,
     norm2_shift,
 ):
+
+    def _supply_all_edge(block_in, vec, array_axis):
+        return lay_the_sources_all(settle_sizes_by_axis(block_in, vec), array_axis)
+
     seq_count, local_len, width = hidden_in.shape
     ctx_count = lax.axis_size("ctx")
     tp_count = lax.axis_size("tp")
@@ -114,7 +138,7 @@
     rest_own = jnp.concatenate(
         [mine(w_out, cols, 0).T, mine(w_up, units, 1), mine(w_down, units, 0).T], axis=1
     )
-    rest_full = lax.all_gather(rest_own, "shard", axis=0, tiled=True)
+    rest_full = _supply_all_edge(rest_own, "shard", 0)
     out_full = rest_full[:, :cols]
     up_full = rest_full[:, cols : cols + units]
     down_full = rest_full[:, cols + units :]

time: 507 us -> 530 us (1.045)
  blocking collectives: 78 us -> 120 us
  waiting for transfers between devices: 301 us -> 275 us
  starting transfers between devices: 0.93 us -> 6.61 us
    all_gather x1, blocking collectives: 21.3 us -> 63.3 us  [shards(): qkv_full = lax.all_gather(qkv_own, 'shard', axis=0, tiled=True)]
    all_gather x1 -> x0, waiting for transfers between devices: 40.8 us -> none  [shards(): rest_full = lax.all_gather(rest_own, 'shard', axis=0, tiled=True)]
    ppermute x0 -> x2, waiting for transfers between devices: none -> 13.2 us  [settle_sizes_by_axis(): lax.ppermute(s_next, axis_name=axis_key, perm=[(p, p ^ r1) for p in range...]
    ppermute x0 -> x2, starting transfers between devices: none -> 5.94 us  [settle_sizes_by_axis(): lax.ppermute(s_next, axis_name=axis_key, perm=[(p, p ^ r1) for p in range...]
  transfers between devices with their start and end apart: 13 -> 14, of which waited for: 11 -> 11; matrix products, arithmetic and copies ran while one was open for 13% -> 11% of each run, Pallas kernels for 0% -> 0%
where the time goes in v1:
time: 530 us; the launch traced here: 529 us
  waiting for transfers between devices  275 us (52%)
  blocking collectives  120 us (23%)
  matrix products  50.6 us (10%)
  local copies, waits for them, and re-layouts  39.8 us (8%)
  other arithmetic  22.7 us (4%)
  between operations  14.8 us (3%)
  starting transfers between devices  6.61 us (1%)
    reduce_scatter x4, waiting for transfers between devices, collect(): lax.psum_scatter(whole, GROUP, scatter_dimension=1, tiled=True)  132 us
    all_gather x3, waiting for transfers between devices, spread(): return lax.all_gather(part, GROUP, axis=1, tiled=True)  76.4 us
    all_gather x1, blocking collectives, shards(): qkv_full = lax.all_gather(qkv_own, 'shard', axis=0, tiled=True)  63.3 us
    reduce_scatter x2, waiting for transfers between devices, owned(): mean = lax.psum_scatter(part, 'shard', scatter_dimension=0, tiled=True)  44.5 us
    psum x1, blocking collectives, shards(): lax.psum(jnp.concatenate([bias_out_grad, gain_one_grad, shift_one_grad, b...  39.4 us
    dot_general x4, matrix products, dot(): return jnp.dot(left, right, preferred_element_type=jnp.float32)  13.9 us
    dot_general x4, matrix products, dot_t(): lax.dot_general(left, right, (((1,), (1,)), ((), ())), preferred_element_...  13.4 us
    ppermute x2, waiting for transfers between devices, settle_sizes_by_axis(): lax.ppermute(s_next, axis_name=axis_key, perm=[(p, p ^ r1) for p in range...  13.2 us
  transfers between devices with their start and end apart: 14, of which 11 were waited for; matrix products, arithmetic and copies ran while one was open for 11% of the time, Pallas kernels for 0%

profile of v1, /device:TPU:0, one launch (start us, length us, event | category | flops | bytes accessed | tf_op | source)
XLA Modules:
  0.0 529.1 jit_solution(11049762568703537847)
XLA Ops:
  9.7 3.1 collective-permute-start
  12.9 13.2 %collective-permute-done = bf16[1,256,1152]{2,1,0:T(8,128)(2,1)S(1)} collective-permute-done((bf16[1,256,1152]{2,1,0:T(8,128)(2,1)S(1)}, bf16[1,256,1152]{2,1,0:T(8,128)(2,1)S(1)}, u32[]{:S(2)}, u32[]{:S(2)}) %collective-permute-start) | collective-permute-done | bytes 589856 | tf_op jit(solution)/shard_map/ppermute | solution.py:22
  26.5 2.8 collective-permute-start.1
  32.3 63.3 %all_gather.33 = bf16[1024,384]{0,1:T(8,128)(2,1)S(1)} all-gather(bf16[256,384]{0,1:T(8,128)(2,1)S(1)} %bitcast.256), channel_id=1, replica_groups=mesh['shard'=4,'ctx'=4,'tp'=2] {'shard'}, dimensions={0}, use_global_device_ids=true | all-gather | bytes 983040 | tf_op jit(solution)/shard_map/all_gather | solution.py:136
  99.3 2.6 add_convert_fusion
  102.2 7.9 %while.45 = (s32[]{:T(128)}, bf16[2,512,2,64]{1,3,2,0:T(8,128)(2,1)S(1)}, f32[2,2,512]{2,1,0:T(2,128)S(1)}, s32[2,512]{1,0:T(2,128)S(1)}, s32[1024]{0:T(1024)S(1...) while((s32[]{:T(128)}, ...), condition=%wide.region_3.4_spmd, body=%wide.region_0.3_spmd.sunk | while | flops 280567808 | bytes 15526005 | solution.py:167
  110.5 3.1 convert_bitcast_fusion.3
  113.6 39.6 %reduce-scatter.7.cloned.1.call-done = bf16[1,128,1024]{2,1,0:T(8,128)(2,1)} async-done(((bf16[1,1024,1024]{2,1,0:T(8,128)(2,1)}), bf16[1,128,1024]{2,1,0:T(8,128)(2,1)}) %reduce-scatter.7.cloned.1.call-update) | async-done | bytes 262160 | tf_op jit(solution)/shard_map/reduce_scatter | solution.py:91
  158.2 27.1 %all-gather.11.cloned.1.call-done = bf16[1,1024,1024]{2,1,0:T(8,128)(2,1)} async-done(((bf16[1,128,1024]{2,1,0:T(8,128)(2,1)}), bf16[1,1024,1024]{2,1,0:T(8,128)(2,1)}) %all-gather.11.cloned.1.call-update) | async-done | bytes 2097168 | tf_op jit(solution)/shard_map/all_gather | solution.py:87
  185.3 4.5 multiply_convert_fusion.1
  190.8 3.8 convert_bitcast_fusion.2
  194.8 41.2 %reduce-scatter.9.cloned.1.call-done = bf16[1,128,1024]{2,1,0:T(8,128)(2,1)} async-done(((bf16[1,1024,1024]{2,1,0:T(8,128)(2,1)}), bf16[1,128,1024]{2,1,0:T(8,128)(2,1)}) %reduce-scatter.9.cloned.1.call-update) | async-done | bytes 262160 | tf_op jit(solution)/shard_map/reduce_scatter | solution.py:91
  239.0 27.7 %all-gather.13.cloned.1.call-done = bf16[1,1024,1024]{2,1,0:T(8,128)(2,1)} async-done(((bf16[1,128,1024]{2,1,0:T(8,128)(2,1)}), bf16[1,1024,1024]{2,1,0:T(8,128)(2,1)}) %all-gather.13.cloned.1.call-update) | async-done | bytes 2097168 | tf_op jit(solution)/shard_map/all_gather | solution.py:87
  266.7 4.5 fusion.115
  272.2 3.8 convert_bitcast_fusion.1
  276.1 41.2 %reduce-scatter.11.cloned.1.call-done = bf16[1,128,1024]{2,1,0:T(8,128)(2,1)} async-done(((bf16[1,1024,1024]{2,1,0:T(8,128)(2,1)}), bf16[1,128,1024]{2,1,0:T(8,128)(2,1)}) %reduce-scatter.11.cloned.1.call-update) | async-done | bytes 262160 | tf_op jit(solution)/shard_map/reduce_scatter | solution.py:91
  321.5 3.3 fusion.72
  327.7 21.6 %all-gather.15.cloned.1.call-done = bf16[1,1024,1024]{2,1,0:T(8,128)(2,1)} async-done(((bf16[1,128,1024]{2,1,0:T(8,128)(2,1)}), bf16[1,1024,1024]{2,1,0:T(8,128)(2,1)}) %all-gather.15.cloned.1.call-update) | async-done | bytes 2097168 | tf_op jit(solution)/shard_map/all_gather | solution.py:87
  349.3 2.3 fusion.81
  352.3 11.8 %while.46 = (s32[]{:T(128)}, f32[1024,2,64]{0,2,1:T(8,128)S(1)}, f32[1024,2,64]{0,2,1:T(8,128)S(1)}, bf16[2,512,2,64]{1,3,2,0:T(8,128)(2,1)S(1)}, bf16[2,512,2,6...) while((s32[]{:T(128)}, f32[1024,2,64]{0,2,1:T(8,128)S(1)}, ...), condition=%wide.region_17.18_spmd.clone, body=%wide.region_15.17_spmd.clone.sunk | while | flops 683998208 | bytes 24283320 | solution.py:250
  369.2 26.7 %reduce-scatter.17.cloned.1.call-done = bf16[256,1024]{0,1:T(8,128)(2,1)} async-done(((bf16[1024,1024]{0,1:T(8,128)(2,1)}), bf16[256,1024]{0,1:T(8,128)(2,1)}) %reduce-scatter.17.cloned.1.call-update) | async-done | bytes 524304 | tf_op jit(solution)/shard_map/reduce_scatter | solution.py:275
  395.9 2.6 convert_bitcast_fusion
  398.6 8.4 %all_gather.36 = bf16[1,256,1024]{2,1,0:T(8,128)(2,1)} all-gather(bf16[1,128,1024]{2,1,0:T(8,128)(2,1)S(1)} %get-tuple-element.301), channel_id=1, replica_groups=mesh['shard'=4,'ctx'=4,'tp'=2] {'tp'}, dimensions={1}, use_global_device_ids=true | all-gather | bytes 786432 | tf_op jit(solution)/shard_map/all_gather | solution.py:199
  407.4 17.9 %reduce-scatter.15.cloned.1.call-done = bf16[256,512]{0,1:T(8,128)(2,1)} async-done(((bf16[1024,512]{0,1:T(8,128)(2,1)}), bf16[256,512]{0,1:T(8,128)(2,1)}) %reduce-scatter.15.cloned.1.call-update) | async-done | bytes 262160 | tf_op jit(solution)/shard_map/reduce_scatter | solution.py:275
  425.3 39.4 %psum.7 = f32[12288]{0:T(1024)S(1)} all-reduce(f32[12288]{0:T(1024)S(1)} %constant_dynamic-update-slice_fusion), channel_id=1, replica_groups=mesh['shard'=4,'ctx'=4,'tp'=2] {'shard','ctx','tp'}, use_global_device_ids=true, to_apply=%region_28.29 | all-reduce | flops 12288 | bytes 98304 | tf_op jit(solution)/shard_map/psum | solution.py:292
  466.6 5.0 reshape.376
  471.6 4.6 slice_bitcast_fusion
  477.9 2.9 copy.47
  480.8 2.2 copy.56
  483.0 9.6 %reduce-scatter.13.cloned.1.call-done = bf16[1,128,1024]{2,1,0:T(8,128)(2,1)} async-done(((bf16[1,1024,1024]{2,1,0:T(8,128)(2,1)}), bf16[1,128,1024]{2,1,0:T(8,128)(2,1)}) %reduce-scatter.13.cloned.1.call-update) | async-done | bytes 262160 | tf_op jit(solution)/shard_map/reduce_scatter | solution.py:91
  493.6 8.7 %all_gather.39 = bf16[1,256,1024]{2,1,0:T(8,128)(2,1)} all-gather(bf16[1,128,1024]{2,1,0:T(8,128)(2,1)S(1)} %add_convert_fusion.1), channel_id=1, replica_groups=mesh['shard'=4,'ctx'=4,'tp'=2] {'tp'}, dimensions={1}, use_global_device_ids=true | all-gather | bytes 786432 | tf_op jit(solution)/shard_map/all_gather | solution.py:269
  502.3 8.6 %all-gather.17.cloned.1.call-done = bf16[1024,512]{0,1:T(8,128)(2,1)} async-done(((bf16[256,512]{0,1:T(8,128)(2,1)}), bf16[1024,512]{0,1:T(8,128)(2,1)}) %all-gather.17.cloned.1.call-update) | async-done | bytes 1048592 | tf_op jit(solution)/shard_map/all_gather | solution.py:276
  (199 shorter events, 68.7 us)
Async XLA Ops:
  7.2 92.1 %all-gather.9.cloned.1.call-start = ((), (), s32[]{:S(2)}) async-start(), calls=%async_computation.6 | async-start | bytes 2621440 | tf_op jit(solution)/shard_map/all_gather | solution.py:137
  9.7 16.4 %collective-permute-start = (bf16[1,256,1152]{2,1,0:T(8,128)(2,1)S(1)}, bf16[1,256,1152]{2,1,0:T(8,128)(2,1)S(1)}, u32[]{:S(2)}, u32[]{:S(2)}) collective-permute-start(bf16[1,256,1152]{2,1,0:T(8,128)(2,1)S(1)} %get-tuple-element.300), channel_id=1, source_target_pairs={{0,8},{8,0},{16,24},{24,16},{1,9},{9,1},{17,25},{25,17},{2,10},{10... | collective-permute-start | bytes 1769480 | tf_op jit(solution)/shard_map/ppermute | solution.py:22
  12.8 140.4 %reduce-scatter.7.cloned.1.call-start = ((), (), s32[]{:S(2)}) async-start(), calls=%async_computation.7 | async-start | bytes 2359296 | tf_op jit(solution)/shard_map/reduce_scatter | solution.py:91
  26.3 3.6 copy-start.11
  26.5 69.1 %collective-permute-start.1 = (bf16[2,256,1152]{2,1,0:T(8,128)(2,1)S(1)}, bf16[2,256,1152]{2,1,0:T(8,128)(2,1)}, u32[]{:S(2)}, u32[]{:S(2)}) collective-permute-start(bf16[2,256,1152]{2,1,0:T(8,128)(2,1)S(1)} %get-tuple-element.295), channel_id=1, source_target_pairs={{0,16},{8,24},{16,0},{24,8},{1,17},{9,25},{17,1},{25,9},{2,18},{10... | collective-permute-start | bytes 3538952 | tf_op jit(solution)/shard_map/ppermute | solution.py:22
  95.6 3.7 copy-start.8
  110.4 42.8 %copy-start.3 = (bf16[1,256,1024]{2,1,0:T(8,128)(2,1)S(1)}, bf16[1,256,1024]{2,1,0:T(8,128)(2,1)}, u32[]{:S(2)}) copy-start(bf16[1,256,1024]{2,1,0:T(8,128)(2,1)} %param.19) | copy-start | bytes 1572868
  110.5 42.8 %copy-start.12 = (f32[1024]{0:T(1024)S(1)}, f32[1024]{0:T(1024)}, u32[]{:S(2)}) copy-start(f32[1024]{0:T(1024)} %param.25) | copy-start | bytes 12292
  113.5 42.0 %copy-start.13 = (f32[1024]{0:T(1024)S(1)}, f32[1024]{0:T(1024)}, u32[]{:S(2)}) copy-start(f32[1024]{0:T(1024)} %param.26) | copy-start | bytes 12292
  113.5 42.0 %copy-start.14 = (f32[1024]{0:T(1024)S(1)}, f32[1024]{0:T(1024)}, u32[]{:S(2)}) copy-start(f32[1024]{0:T(1024)} %param.27) | copy-start | bytes 12292
  113.6 71.8 %all-gather.11.cloned.1.call-start = ((), (), s32[]{:S(2)}) async-start(), calls=%async_computation.8 | async-start | bytes 2359296 | tf_op jit(solution)/shard_map/all_gather | solution.py:87
  157.4 78.6 %reduce-scatter.9.cloned.1.call-start = ((), (), s32[]{:S(2)}) async-start(), calls=%async_computation.9 | async-start | bytes 2359296 | tf_op jit(solution)/shard_map/reduce_scatter | solution.py:91
  194.7 41.3 %copy-start.2 = (bf16[1,128,1024]{2,1,0:T(8,128)(2,1)S(1)}, bf16[1,128,1024]{2,1,0:T(8,128)(2,1)}, u32[]{:S(2)}) copy-start(bf16[1,128,1024]{2,1,0:T(8,128)(2,1)} %reduce-scatter.7.cloned.1.call-done) | copy-start | bytes 786436
  194.7 41.3 %copy-start.16 = (f32[1024]{0:T(1024)S(1)}, f32[1024]{0:T(1024)}, u32[]{:S(2)}) copy-start(f32[1024]{0:T(1024)} %param.31) | copy-start | bytes 12292
  194.7 42.8 %copy-start.10 = (bf16[1,256,1024]{2,1,0:T(8,128)(2,1)S(1)}, bf16[1,256,1024]{2,1,0:T(8,128)(2,1)}, u32[]{:S(2)}) copy-start(bf16[1,256,1024]{2,1,0:T(8,128)(2,1)} %param.20) | copy-start | bytes 1572868
  194.7 42.8 %copy-start.15 = (f32[1024]{0:T(1024)S(1)}, f32[1024]{0:T(1024)}, u32[]{:S(2)}) copy-start(f32[1024]{0:T(1024)} %param.32) | copy-start | bytes 12292
  194.7 43.1 %copy-start.17 = (f32[1024]{0:T(1024)S(1)}, f32[1024]{0:T(1024)}, u32[]{:S(2)}) copy-start(f32[1024]{0:T(1024)} %param.33) | copy-start | bytes 12292
  194.7 72.0 %all-gather.13.cloned.1.call-start = ((), (), s32[]{:S(2)}) async-start(), calls=%async_computation.10 | async-start | bytes 2359296 | tf_op jit(solution)/shard_map/all_gather | solution.py:87
  238.7 78.5 %reduce-scatter.11.cloned.1.call-start = ((), (), s32[]{:S(2)}) async-start(), calls=%async_computation.11 | async-start | bytes 2359296 | tf_op jit(solution)/shard_map/reduce_scatter | solution.py:91
  276.0 73.3 %all-gather.15.cloned.1.call-start = ((), (), s32[]{:S(2)}) async-start(), calls=%async_computation.12 | async-start | bytes 2359296 | tf_op jit(solution)/shard_map/all_gather | solution.py:87
  321.4 74.4 %reduce-scatter.17.cloned.1.call-start = ((), (), s32[]{:S(2)}) async-start(), calls=%async_computation.15 | async-start | bytes 2621440 | tf_op jit(solution)/shard_map/reduce_scatter | solution.py:275
  321.5 3.3 copy-start.19
  321.5 3.3 copy-start.22
  327.7 97.6 %reduce-scatter.15.cloned.1.call-start = ((), (), s32[]{:S(2)}) async-start(), calls=%async_computation.14 | async-start | bytes 1310720 | tf_op jit(solution)/shard_map/reduce_scatter | solution.py:275
  368.1 27.9 %copy-start.9 = (bf16[1024,384]{0,1:T(8,128)(2,1)S(1)}, bf16[1024,384]{0,1:T(8,128)(2,1)}, u32[]{:S(2)}) copy-start(bf16[1024,384]{0,1:T(8,128)(2,1)} %copy-done.8) | copy-start | bytes 2359300
  369.1 97.4 %all-gather.19.cloned.1.call-start = ((), (), s32[]{:S(2)}) async-start(), calls=%async_computation.17 | async-start | bytes 2621440 | tf_op jit(solution)/shard_map/all_gather | solution.py:276
  395.9 96.7 %reduce-scatter.13.cloned.1.call-start = ((), (), s32[]{:S(2)}) async-start(), calls=%async_computation.13 | async-start | bytes 2359296 | tf_op jit(solution)/shard_map/reduce_scatter | solution.py:91
  398.6 112.2 %all-gather.17.cloned.1.call-start = ((), (), s32[]{:S(2)}) async-start(), calls=%async_computation.16 | async-start | bytes 1310720 | tf_op jit(solution)/shard_map/all_gather | solution.py:276
  480.8 11.8 %copy-start.5 = (f32[1,128,1024]{2,1,0:T(8,128)S(1)}, f32[1,128,1024]{2,1,0:T(8,128)}, u32[]{:S(2)}) copy-start(f32[1,128,1024]{2,1,0:T(8,128)} %copy-done.4) | copy-start | bytes 1572868
  516.9 3.8 copy-start.6
  516.9 5.4 %copy-start.1 = (bf16[256,2048]{1,0:T(8,128)(2,1)S(1)}, bf16[256,2048]{1,0:T(8,128)(2,1)}, u32[]{:S(2)}) copy-start(bf16[256,2048]{1,0:T(8,128)(2,1)} %param.28) | copy-start | bytes 3145732
  518.7 2.8 copy-start.7
  (5 other events, 6.4 us)
Sparse Core Ops, SparseCore 0:
  13.0 22.7 all-gather.8
  113.7 39.5 reduce-scatter.6
  157.5 27.7 all-gather.10
  194.8 41.0 reduce-scatter.8
  238.9 27.7 all-gather.12
  276.1 41.0 reduce-scatter.10
  321.5 27.7 all-gather.14
  352.2 43.6 reduce-scatter.16
  398.7 26.4 reduce-scatter.14
  426.7 21.4 all-gather.18
  451.4 41.0 reduce-scatter.12
  494.0 16.8 all-gather.16
